TPU v7x, 128 devices: a whole 4x4x4 slice. The times are simulated.
128 devices in a mesh: ctx: 16 (over z_hi, x, core), tp: 8 (over z_lo, y).
Axes of the slice: x: 4, y: 4, z: 4 (z_hi: 2, z_lo: 2; z = z_hi * 2 + z_lo), core: 2. Of those that a mesh axis runs over, the one named last changes fastest.
Arguments:
- query_gate: bfloat16 [32, 1048576], P('tp', 'ctx'), may hold values from -6 to 6
- key_branch: bfloat16 [32, 1048576], P('tp', 'ctx'), may hold values from -6 to 6
- value_branch: bfloat16 [32, 1048576], P('tp', 'ctx'), may hold values from -6 to 6
- long_filter: float32 [32, 1048576], P('tp', 'ctx'), may hold values from -0.005859375 to 0.005859375
- skip_gain: float32 [32], P('tp'), may hold values from 0.5 to 1.5
- out_weight: bfloat16 [32, 32], replicated, may hold values from -1 to 1
Outputs:
- mixed: bfloat16 [32, 1048576], P('tp', 'ctx')
All inputs are finite; a program needn't handle non-finite values.
Results may differ from a plain program's by a relative error of at most 0.02.
Values may be sent and summed in bfloat16 or wider, within the bound.
A program may use at most 256 MiB of HBM per device.

v0:
```python
import math
import jax
import jax.numpy as jnp
from jax import lax
from jax.sharding import PartitionSpec as P

FACTOR = 128


def turn_table(left_idx, right_idx, length, sign):
    phase = left_idx[:, None] * right_idx[None, :] % length
    angle = sign * 2.0 * math.pi / length * phase.astype(jnp.float32)
    return (jnp.cos(angle), jnp.sin(angle))


def apply_form(form, table, values):
    return jnp.einsum(form, table, values, precision=lax.Precision.HIGHEST)


def apply_complex(form, tab_re, tab_im, val_re, val_im, table_first):
    if table_first:
        out_re = apply_form(form, tab_re, val_re) - apply_form(form, tab_im, val_im)
        out_im = apply_form(form, tab_re, val_im) + apply_form(form, tab_im, val_re)
    else:
        out_re = apply_form(form, val_re, tab_re) - apply_form(form, val_im, tab_im)
        out_im = apply_form(form, val_im, tab_re) + apply_form(form, val_re, tab_im)
    return (out_re, out_im)


def times_table(val_re, val_im, tab_re, tab_im):
    return (val_re * tab_re - val_im * tab_im, val_re * tab_im + val_im * tab_re)


def local_forward(val_re, val_im, width_a, width_b):
    iota_a = jnp.arange(width_a, dtype=jnp.int32)
    iota_b = jnp.arange(width_b, dtype=jnp.int32)
    fb_re, fb_im = turn_table(iota_b, iota_b, width_b, -1.0)
    step_re, step_im = apply_complex("cb,...ba->...ca", fb_re, fb_im, val_re, val_im, True)
    tw_re, tw_im = turn_table(iota_b, iota_a, width_a * width_b, -1.0)
    step_re, step_im = times_table(step_re, step_im, tw_re, tw_im)
    fa_re, fa_im = turn_table(iota_a, iota_a, width_a, -1.0)
    return apply_complex("...ca,ad->...cd", fa_re, fa_im, step_re, step_im, False)


def local_inverse(val_re, val_im, width_a, width_b):
    iota_a = jnp.arange(width_a, dtype=jnp.int32)
    iota_b = jnp.arange(width_b, dtype=jnp.int32)
    fa_re, fa_im = turn_table(iota_a, iota_a, width_a, 1.0)
    step_re, step_im = apply_complex("...cd,da->...ca", fa_re, fa_im, val_re, val_im, False)
    tw_re, tw_im = turn_table(iota_b, iota_a, width_a * width_b, 1.0)
    step_re, step_im = times_table(step_re, step_im, tw_re, tw_im)
    fb_re, fb_im = turn_table(iota_b, iota_b, width_b, 1.0)
    return apply_complex("bc,...ca->...ba", fb_re, fb_im, step_re, step_im, True)


def local(query_gate, key_branch, value_branch, long_filter, skip_gain, out_weight):
    ctx_count = lax.axis_size("ctx")
    ctx_index = lax.axis_index("ctx")
    chans, tok_count = query_gate.shape
    width_a = FACTOR
    width_b = tok_count // FACTOR
    residues = 2 * ctx_count
    fft_length = residues * tok_count
    signal = key_branch.astype(jnp.float32) * value_branch.astype(jnp.float32)
    stacked = jnp.concatenate([signal, long_filter], 0)[:, None, :]
    blocks = lax.all_to_all(
        stacked.astype(jnp.bfloat16), "ctx", split_axis=2, concat_axis=1, tiled=True
    ).astype(stacked.dtype)
    dev_idx = jnp.arange(ctx_count, dtype=jnp.int32)
    second_res = jnp.where(dev_idx == 0, ctx_count, residues - dev_idx)
    res_order = jnp.stack([dev_idx, second_res], 1).reshape(residues)
    blk_idx = jnp.arange(ctx_count, dtype=jnp.int32)
    cross_re, cross_im = turn_table(res_order, blk_idx, residues, -1.0)
    spec_re = apply_form("kn,snm->skm", cross_re, blocks)
    spec_im = apply_form("kn,snm->skm", cross_im, blocks)
    spec_re, spec_im = (
        lax.all_to_all(
            spec_re.astype(jnp.bfloat16), "ctx", split_axis=1, concat_axis=2, tiled=True
        ).astype(spec_re.dtype),
        lax.all_to_all(
            spec_im.astype(jnp.bfloat16), "ctx", split_axis=1, concat_axis=2, tiled=True
        ).astype(spec_im.dtype),
    )
    own_res = jnp.stack([ctx_index, jnp.where(ctx_index == 0, ctx_count, residues - ctx_index)])
    offsets = jnp.arange(tok_count, dtype=jnp.int32)
    tw_re, tw_im = turn_table(own_res, offsets, fft_length, -1.0)
    spec_re, spec_im = times_table(spec_re, spec_im, tw_re, tw_im)
    series = spec_re.shape[0]
    spec_re = spec_re.reshape(series, 2, width_b, width_a)
    spec_im = spec_im.reshape(series, 2, width_b, width_a)
    spec_re, spec_im = local_forward(spec_re, spec_im, width_a, width_b)
    sig_re, sig_im = (spec_re[:chans], spec_im[:chans])
    fil_re, fil_im = (spec_re[chans:], spec_im[chans:])
    prod_re, prod_im = times_table(sig_re, sig_im, fil_re, fil_im)
    back_re, back_im = local_inverse(prod_re, prod_im, width_a, width_b)
    back_re = back_re.reshape(chans, 2, tok_count)
    back_im = back_im.reshape(chans, 2, tok_count)
    inv_re, inv_im = turn_table(own_res, offsets, fft_length, 1.0)
    back_re, back_im = times_table(back_re, back_im, inv_re, inv_im)
    back_re = back_re * (1.0 / fft_length)
    back_im = back_im * (1.0 / fft_length)
    block_rows = jnp.arange(1 * lax.axis_size("ctx"), dtype=jnp.int32)
    row_re, row_im = turn_table(block_rows, own_res, residues, 1.0)
    conv = lax.psum_scatter(
        (
            apply_form("nj,cjm->ncm", row_re, back_re) - apply_form("nj,cjm->ncm", row_im, back_im)
        ).astype(jnp.bfloat16),
        "ctx",
        scatter_dimension=0,
        tiled=True,
    ).astype(jnp.float32)[0]
    gated = (query_gate.astype(jnp.float32) * (conv + skip_gain[:, None] * signal)).astype(
        jnp.bfloat16
    )
    tp_index = lax.axis_index("tp")
    out_dev = out_weight.shape[1] // lax.axis_size("tp")
    own_cols = lax.dynamic_slice_in_dim(out_weight, tp_index * out_dev, out_dev, 1)
    mixed = jnp.dot(
        own_cols.T,
        lax.all_gather(gated, "tp", axis=0, tiled=True),
        preferred_element_type=jnp.float32,
    )
    return mixed.astype(jnp.bfloat16)


def solution(mesh):
    placed = (P("tp", "ctx"), P("tp", "ctx"), P("tp", "ctx"), P("tp", "ctx"), P("tp"), P())
    return jax.shard_map(
        local, mesh=mesh, in_specs=placed, out_specs=P("tp", "ctx"), check_vma=False
    )
```

profile of v0, /device:TPU:1, one launch (start us, length us, event | category | flops | bytes accessed | tf_op | source)
XLA Modules:
  0.0 1102.9 jit_solution(4058956443266954925)
XLA Ops:
  6.5 2.0 fusion.52
  8.5 0.5 pad_maximum_fusion
  9.1 49.8 %copy.64 = bf16[8,1,65536]{0,1,2:T(2,128)(2,1)} copy(bf16[8,1,65536]{2,0,1:T(8,128)(2,1)S(1)} %pad_maximum_fusion) | data formatting | bytes 2097152 | tf_op jit(solution)/shard_map/concatenate | solution.py:65
  58.9 0.5 broadcast.406
  59.4 355.8 %reduce = bf16[65536,8]{1,0:T(8,128)(2,1)} reduce(bf16[65536,1,8]{2,1,0:T(2,128)(2,1)} %bitcast.149, bf16[]{:T(256)} %broadcast.406), dimensions={1}, to_apply=%bitcast.134.reduce_sub_computation | reduce | bytes 2097154
  415.2 20.6 %reshape.239 = bf16[16,2,16384]{2,1,0:T(2,128)(2,1)} reshape(bf16[65536,8]{1,0:T(8,128)(2,1)} %reduce) | data formatting | bytes 2097152
  435.8 9.4 all-to-all-start
  445.3 0.1 copy.66
  445.3 0.1 mul.566
  445.4 17.1 %all-to-all-done = bf16[16,2,16384]{2,1,0:T(2,128)(2,1)S(1)} async-done(((bf16[16,2,16384]{2,1,0:T(2,128)(2,1)}), bf16[16,2,16384]{2,1,0:T(2,128)(2,1)S(1)}, u32[]{:S(2)}, u32[]{:S(2)}) %all-to-all-start) | async-done | bytes 1048608 | tf_op jit(solution)/shard_map/all_to_all | solution.py:66
  462.5 39.4 %reshape.240 = bf16[65536,1,8]{2,1,0:T(2,128)(2,1)} reshape(bf16[16,2,16384]{2,1,0:T(2,128)(2,1)S(1)} %all-to-all-done) | data formatting | bytes 2097152
  501.9 58.6 %copy.65 = bf16[8,1,65536]{2,0,1:T(8,128)(2,1)S(1)} copy(bf16[8,1,65536]{0,1,2:T(2,128)(2,1)} %bitcast.150) | data formatting | bytes 2097152 | tf_op jit(solution)/shard_map/all_to_all | solution.py:66
  560.5 2.0 fusion.2
  562.5 2.5 copy.69
  565.0 4.2 all-to-all-start.2
  569.2 0.1 pad_add_fusion.1
  569.3 2.0 fusion.1
  571.3 2.6 copy.67
  573.9 24.0 %all-to-all-done.2 = bf16[8,32,4096]{2,0,1:T(8,128)(2,1)S(1)} async-done(((bf16[8,32,4096]{2,0,1:T(8,128)(2,1)}), bf16[8,32,4096]{2,0,1:T(8,128)(2,1)S(1)}, u32[]{:S(2)}, u32[]{:S(2)}) %all-to-all-start.2) | async-done | bytes 2097184 | tf_op jit(solution)/shard_map/all_to_all | solution.py:80
  597.9 5.5 all-to-all-start.1
  603.4 0.2 all-reduce.3.cloned.1.call-start
  603.7 8.9 fusion.77
  612.5 1.0 multiply_sine_fusion.6
  613.5 0.9 copy.80
  614.4 1.0 multiply_cosine_fusion.6
  615.3 0.8 copy.79
  616.2 1.7 multiply_sine_fusion.7
  617.9 2.1 fusion.81
  620.0 4.8 copy.119
  624.9 4.9 reshape.220
  629.7 2.4 all-to-all-done.1
  632.1 4.8 copy.120
  636.9 5.3 reshape.219
  642.2 21.0 %fusion.34 = f32[8,2,128,512]{3,2,1,0:T(8,128)S(1)} fusion(f32[8,2,512,128]{3,2,1,0:T(8,128)} %reshape.220, f32[8,2,512,128]{3,2,1,0:T(8,128)} %reshape.219, f32[2,512,128]{2,1,0:T(8,128)S(1)} %get-tuple-element.8, f32[2,512,128]{2,1,0:T(8,128)S(1)} %get-tuple-element.7), kind=kOutput, calls=%fused_computation.61 | convolution fusion | flops 6449266688 | bytes 13631488 | tf_op jit(solution)/shard_map/cb,...ba->...ca/dot_general | solution.py:17
  663.3 17.3 %fusion.36 = f32[8,2,128,512]{3,2,1,0:T(8,128)S(1)} fusion(f32[8,2,512,128]{3,2,1,0:T(8,128)S(1)} %copy-done.1, f32[8,2,512,128]{3,2,1,0:T(8,128)S(1)} %copy-done.2, f32[2,512,128]{2,1,0:T(8,128)S(1)} %get-tuple-element.8, f32[2,512,128]{2,1,0:T(8,128)S(1)} %get-tuple-element.7), kind=kOutput, calls=%fused_computation.63 | convolution fusion | flops 6449266688 | bytes 13631488 | tf_op jit(solution)/shard_map/cb,...ba->...ca/dot_general | solution.py:17
  680.5 17.7 %convolution_add_fusion.1 = f32[8,2,128,512]{3,2,1,0:T(8,128)S(1)} fusion(f32[8,2,128,512]{3,2,1,0:T(8,128)S(1)} %fusion.34, f32[8,2,512,128]{3,2,1,0:T(8,128)S(1)} %copy-done.1, f32[8,2,512,128]{3,2,1,0:T(8,128)S(1)} %copy-done.2, f32[2,512,128]{2,1,0:T(8,128)S(1)} %get-tuple-element.8, f32[2,512,128]{2,1,0:T(8,128)S(1)} %get-tuple-element.7), kind=kOutput, calls=%fused_computation.19 | convolution fusion | flops 6450315264 | bytes 17825792 | tf_op jit(solution)/shard_map/cb,...ba->...ca/dot_general | solution.py:17
  698.2 17.3 %convolution_subtract_fusion.2 = f32[8,2,128,512]{3,2,1,0:T(8,128)S(1)} fusion(f32[8,2,128,512]{3,2,1,0:T(8,128)S(1)} %fusion.36, f32[8,2,512,128]{3,2,1,0:T(8,128)S(1)} %copy-done.1, f32[8,2,512,128]{3,2,1,0:T(8,128)S(1)} %copy-done.2, f32[2,512,128]{2,1,0:T(8,128)S(1)} %get-tuple-element.8, f32[2,512,128]{2,1,0:T(8,128)S(1)} %get-tuple-element.7), kind=kOutput, calls=%fused_computation.20 | convolution fusion | flops 6450315264 | bytes 17825792 | tf_op jit(solution)/shard_map/cb,...ba->...ca/dot_general | solution.py:17
  715.6 7.6 fusion.14
  723.2 7.4 fusion.18
  730.6 7.2 convolution_add_fusion
  737.8 7.4 convolution_subtract_fusion.1
  745.3 0.5 multiply_subtract_fusion.2
  745.8 2.1 fusion.87
  747.9 2.1 fusion.89
  750.1 2.1 convolution_add_fusion.2
  752.2 2.5 convolution_subtract_fusion.3
  754.7 10.6 fusion.28
  765.3 11.8 %fusion.30 = f32[4,2,128,512]{3,2,1,0:T(8,128)} fusion(f32[4,2,512,128]{3,2,1,0:T(8,128)S(1)} %convolution_add_fusion.2, f32[4,2,512,128]{3,2,1,0:T(8,128)S(1)} %convolution_subtract_fusion.3, f32[512,128]{1,0:T(8,128)S(1)} %copy-done.8, f32[512,128]{1,0:T(8,128)S(1)} %copy-done.9), kind=kOutput, calls=%fused_computation.57 | convolution fusion | flops 3226468352 | bytes 6815744 | tf_op jit(solution)/shard_map/bc,...ca->...ba/dot_general | solution.py:17
  777.1 12.0 %add_bitcast_fusion = f32[4,2,512,128]{2,3,1,0:T(8,128)} fusion(f32[4,2,128,512]{3,2,1,0:T(8,128)S(1)} %fusion.28, f32[4,2,512,128]{3,2,1,0:T(8,128)S(1)} %convolution_add_fusion.2, f32[4,2,512,128]{3,2,1,0:T(8,128)S(1)} %convolution_subtract_fusion.3, f32[512,128]{1,0:T(8,128)S(1)} %copy-done.8, f32[512,128]{1,0:T(8,128)S(1)} %copy-done.9), kind=kOutput, calls=%fused_computation.29 | convolution fusion | flops 3226992640 | bytes 8912896 | tf_op jit(solution)/shard_map/bc,...ca->...ba/dot_general | solution.py:17
  789.1 3.0 copy.86
  792.1 4.4 reshape.218
  796.5 14.4 %subtract_bitcast_fusion = f32[4,2,512,128]{2,3,1,0:T(8,128)} fusion(f32[4,2,128,512]{3,2,1,0:T(8,128)} %fusion.30, f32[4,2,512,128]{3,2,1,0:T(8,128)S(1)} %convolution_add_fusion.2, f32[4,2,512,128]{3,2,1,0:T(8,128)} %copy-done.3, f32[512,128]{1,0:T(8,128)S(1)} %copy-done.8, f32[512,128]{1,0:T(8,128)} %copy.79), kind=kOutput, calls=%fused_computation.31 | convolution fusion | flops 3226992640 | bytes 8912896 | tf_op jit(solution)/shard_map/bc,...ca->...ba/dot_general | solution.py:17
  810.9 3.0 copy.83
  813.9 4.4 reshape.217
  818.3 17.5 %fusion.9 = f32[16,4,65536]{2,0,1:T(8,128)S(1)} fusion(f32[4,2,65536]{2,1,0:T(2,128)S(1)} %copy-done.4, f32[4,2,65536]{2,1,0:T(2,128)} %reshape.217, f32[2,65536]{1,0:T(2,128)S(1)} %get-tuple-element.10, f32[2,65536]{1,0:T(2,128)S(1)} %get-tuple-element.9, s32[2]{0:T(128)S(1)} %pad_add_fusion.1), kind=kOutput, calls=%fused_computation.25 | convolution fusion | flops 102760896 | bytes 22020104 | tf_op jit(solution)/shard_map/nj,cjm->ncm/dot_general | solution.py:17
  835.8 18.1 %fusion = bf16[16,4,65536]{2,0,1:T(8,128)(2,1)S(1)} fusion(f32[16,4,65536]{2,0,1:T(8,128)S(1)} %fusion.9, f32[4,2,65536]{2,1,0:T(2,128)S(1)} %copy-done.4, f32[4,2,65536]{2,1,0:T(2,128)S(1)} %copy-done.5, f32[2,65536]{1,0:T(2,128)S(1)} %get-tuple-element.10, f32[2,65536]{1,0:T(2,128)S(1)} %get-tuple-element.9, s32[2]{0:T(128)S(1)} %pad_add_fusion.1), kind=kOutput, calls=%fused_computation.1 | convolution fusion | flops 111149504 | bytes 30408712 | tf_op jit(solution)/shard_map/nj,cjm->ncm/dot_general | solution.py:17
  853.9 13.0 %copy.87 = bf16[16,4,65536]{2,1,0:T(4,128)(2,1)} copy(bf16[16,4,65536]{2,0,1:T(8,128)(2,1)S(1)} %fusion) | data formatting | bytes 16777216 | tf_op jit(solution)/shard_map/convert_element_type | solution.py:107
  867.0 0.6 copy-done.14
  867.5 0.7 dynamic-slice
  868.2 160.8 %all-reduce.3.cloned.1.call-done = bf16[16,4,65536]{2,1,0:T(4,128)(2,1)} async-done(((bf16[16,4,65536]{2,1,0:T(4,128)(2,1)}), bf16[16,4,65536]{2,1,0:T(4,128)(2,1)}) %all-reduce.3.cloned.1.call-update) | async-done | bytes 8388624
  1029.0 3.3 fusion.56
  1032.4 54.5 %all-gather.3.cloned.1.call-done = bf16[8,4,65536]{2,1,0:T(4,128)(2,1)} async-done(((bf16[1,4,65536]{2,1,0:T(4,128)(2,1)}), bf16[8,4,65536]{2,1,0:T(4,128)(2,1)}) %all-gather.3.cloned.1.call-update) | async-done | bytes 4194320 | tf_op jit(solution)/shard_map/all_gather | solution.py:120
  1086.8 5.2 reshape.225
  1092.0 3.8 convolution_convert_fusion
  (36 shorter events, 0.2 us)
Async XLA Ops:
  6.5 1085.5 %copy-start = (bf16[32,32]{1,0:T(8,128)(2,1)S(1)}, bf16[32,32]{1,0:T(8,128)(2,1)}, u32[]{:S(2)}) copy-start(bf16[32,32]{1,0:T(8,128)(2,1)} %param.11) | copy-start | bytes 6148
  435.8 26.7 %all-to-all-start = ((bf16[16,2,16384]{2,1,0:T(2,128)(2,1)}), bf16[16,2,16384]{2,1,0:T(2,128)(2,1)S(1)}, u32[]{:S(2)}, u32[]{:S(2)}) async-start(bf16[16,2,16384]{2,1,0:T(2,128)(2,1)} %reshape.239), calls=%async_computation | async-start | bytes 2097152 | tf_op jit(solution)/shard_map/all_to_all | solution.py:66
  565.0 32.9 %all-to-all-start.2 = ((bf16[8,32,4096]{2,0,1:T(8,128)(2,1)}), bf16[8,32,4096]{2,0,1:T(8,128)(2,1)S(1)}, u32[]{:S(2)}, u32[]{:S(2)}) async-start(bf16[8,32,4096]{2,0,1:T(8,128)(2,1)} %copy.69), calls=%async_computation.2 | async-start | bytes 4194304 | tf_op jit(solution)/shard_map/all_to_all | solution.py:80
  597.9 18.3 %copy-start.6 = (bf16[8,32,4096]{2,0,1:T(8,128)(2,1)}, bf16[8,32,4096]{2,0,1:T(8,128)(2,1)S(1)}, u32[]{:S(2)}) copy-start(bf16[8,32,4096]{2,0,1:T(8,128)(2,1)S(1)} %all-to-all-done.2) | copy-start | bytes 6291460
  597.9 34.2 %all-to-all-start.1 = ((bf16[8,32,4096]{2,0,1:T(8,128)(2,1)}), bf16[8,32,4096]{2,0,1:T(8,128)(2,1)}, u32[]{:S(2)}, u32[]{:S(2)}) async-start(bf16[8,32,4096]{2,0,1:T(8,128)(2,1)} %copy.67), calls=%async_computation.1 | async-start | bytes 4194304 | tf_op jit(solution)/shard_map/all_to_all | solution.py:77
  603.4 425.6 %all-reduce.3.cloned.1.call-start = ((), (), s32[]{:S(2)}) async-start(), calls=%async_computation.4 | async-start | bytes 16777216
  642.2 21.0 %copy-start.1 = (f32[8,2,512,128]{3,2,1,0:T(8,128)S(1)}, f32[8,2,512,128]{3,2,1,0:T(8,128)}, u32[]{:S(2)}) copy-start(f32[8,2,512,128]{3,2,1,0:T(8,128)} %reshape.220) | copy-start | bytes 12582916
  642.2 21.0 %copy-start.2 = (f32[8,2,512,128]{3,2,1,0:T(8,128)S(1)}, f32[8,2,512,128]{3,2,1,0:T(8,128)}, u32[]{:S(2)}) copy-start(f32[8,2,512,128]{3,2,1,0:T(8,128)} %reshape.219) | copy-start | bytes 12582916
  698.2 17.4 %copy-start.7 = (f32[512,128]{0,1:T(8,128)S(1)}, f32[512,128]{0,1:T(8,128)}, u32[]{:S(2)}) copy-start(f32[512,128]{0,1:T(8,128)} %get-tuple-element.14) | copy-start | bytes 786436
  752.2 2.5 copy-start.8
  752.2 2.5 copy-start.9
  754.7 22.4 %copy-start.3 = (f32[4,2,512,128]{3,2,1,0:T(8,128)}, f32[4,2,512,128]{3,2,1,0:T(8,128)S(1)}, u32[]{:S(2)}) copy-start(f32[4,2,512,128]{3,2,1,0:T(8,128)S(1)} %convolution_subtract_fusion.3) | copy-start | bytes 6291460
  810.9 7.4 copy-start.4
  818.3 17.5 %copy-start.5 = (f32[4,2,65536]{2,1,0:T(2,128)S(1)}, f32[4,2,65536]{2,1,0:T(2,128)}, u32[]{:S(2)}) copy-start(f32[4,2,65536]{2,1,0:T(2,128)} %reshape.217) | copy-start | bytes 6291460
  866.9 0.7 copy-start.14
  866.9 162.1 %copy-start.10 = (bf16[4,65536]{1,0:T(4,128)(2,1)S(1)}, bf16[4,65536]{1,0:T(4,128)(2,1)}, u32[]{:S(2)}) copy-start(bf16[4,65536]{1,0:T(4,128)(2,1)} %param.8) | copy-start | bytes 1572868
  866.9 162.1 %copy-start.11 = (bf16[4,65536]{1,0:T(4,128)(2,1)S(1)}, bf16[4,65536]{1,0:T(4,128)(2,1)}, u32[]{:S(2)}) copy-start(bf16[4,65536]{1,0:T(4,128)(2,1)} %param.7) | copy-start | bytes 1572868
  866.9 162.1 %copy-start.12 = (bf16[4,65536]{1,0:T(4,128)(2,1)S(1)}, bf16[4,65536]{1,0:T(4,128)(2,1)}, u32[]{:S(2)}) copy-start(bf16[4,65536]{1,0:T(4,128)(2,1)} %param.6) | copy-start | bytes 1572868
  866.9 162.1 %copy-start.13 = (f32[4]{0:T(128)S(1)}, f32[4]{0:T(128)}, u32[]{:S(2)}) copy-start(f32[4]{0:T(128)} %param.10) | copy-start | bytes 52
  866.9 219.9 %all-gather.3.cloned.1.call-start = ((), (), s32[]{:S(2)}) async-start(), calls=%async_computation.3 | async-start | bytes 4718592 | tf_op jit(solution)/shard_map/all_gather | solution.py:120
Sparse Core Ops, SparseCore 0:
  867.0 161.9 all-reduce.2
  1032.5 54.2 all-gather.2
where the time goes:
time: 1110 us; the launch traced here: 1100 us
  other arithmetic  377 us (34%)
  waiting for transfers between devices  259 us (23%)
  local copies, waits for them, and re-layouts  230 us (21%)
  matrix products  204 us (18%)
  starting transfers between devices  19.4 us (2%)
  between operations  14 us (1%)
    unnamed x2, other arithmetic  359 us
    dot_general x20, matrix products, apply_form(): return jnp.einsum(form, table, values, precision=lax.Precision.HIGHEST)  200 us
    unnamed x3, waiting for transfers between devices  161 us
    unnamed x35, local copies, waits for them, and re-layouts  67 us
    all_to_all x1, local copies, waits for them, and re-layouts, local(): lax.all_to_all(stacked.astype(jnp.bfloat16), 'ctx', split_axis=2, concat_...  58.6 us
    all_gather x1, waiting for transfers between devices, local(): lax.all_gather(gated, 'tp', axis=0, tiled=True)  54.5 us
    concatenate x1, local copies, waits for them, and re-layouts, local(): stacked = jnp.concatenate([signal, long_filter], 0)[:, None, :]  49.8 us
    all_to_all x1, waiting for transfers between devices, local(): lax.all_to_all(spec_im.astype(jnp.bfloat16), 'ctx', split_axis=1, concat_...  24 us
  transfers between devices with their start and end apart: 5, of which 5 were waited for; matrix products, arithmetic and copies ran while one was open for 3% of the time, Pallas kernels for 0%

commit v1 on v0

--- a/solution.py
+++ b/solution.py
@@ -5,6 +5,12 @@
 from jax.sharding import PartitionSpec as P
 
 FACTOR = 128
+
+
+def exchange_blocks(x, axis, split, join):
+    cells = jnp.split(x, lax.axis_size(axis), axis=split)
+    received = lax.all_to_all(jnp.stack(cells), axis, 0, 0)
+    return jnp.concatenate(received, axis=join)
 
 
 def turn_table(left_idx, right_idx, length, sign):
@@ -63,9 +69,7 @@
     fft_length = residues * tok_count
     signal = key_branch.astype(jnp.float32) * value_branch.astype(jnp.float32)
     stacked = jnp.concatenate([signal, long_filter], 0)[:, None, :]
-    blocks = lax.all_to_all(
-        stacked.astype(jnp.bfloat16), "ctx", split_axis=2, concat_axis=1, tiled=True
-    ).astype(stacked.dtype)
+    blocks = exchange_blocks(stacked.astype(jnp.bfloat16), "ctx", 2, 1).astype(stacked.dtype)
     dev_idx = jnp.arange(ctx_count, dtype=jnp.int32)
     second_res = jnp.where(dev_idx == 0, ctx_count, residues - dev_idx)
     res_order = jnp.stack([dev_idx, second_res], 1).reshape(residues)

time: 1110 us -> 595 us (0.54)
  other arithmetic: 377 us -> 31 us
  local copies, waits for them, and re-layouts: 230 us -> 60.7 us
    unnamed x2 -> x16, other arithmetic: 359 us -> 13.1 us
    unnamed x35 -> x32, local copies, waits for them, and re-layouts: 67 us -> 6.44 us
    all_to_all x1 -> x0, local copies, waits for them, and re-layouts: 58.6 us -> none  [local(): lax.all_to_all(stacked.astype(jnp.bfloat16), 'ctx', split_axis=2, concat_...]
    concatenate x1 -> x0, local copies, waits for them, and re-layouts: 49.8 us -> none  [local(): stacked = jnp.concatenate([signal, long_filter], 0)[:, None, :]]
    all_to_all x1, waiting for transfers between devices: 24 us -> 2.04 us  [local(): lax.all_to_all(spec_im.astype(jnp.bfloat16), 'ctx', split_axis=1, concat_...]
    all_to_all x1, waiting for transfers between devices: 2.35 us -> 24.1 us  [local(): lax.all_to_all(spec_re.astype(jnp.bfloat16), 'ctx', split_axis=1, concat_...]
  transfers between devices with their start and end apart: 5 -> 5, of which waited for: 5 -> 5; matrix products, arithmetic and copies ran while one was open for 3% -> 5% of each run, Pallas kernels for 0% -> 0%
where the time goes in v1:
time: 595 us; the launch traced here: 588 us
  waiting for transfers between devices  259 us (44%)
  matrix products  204 us (34%)
  local copies, waits for them, and re-layouts  60.7 us (10%)
  other arithmetic  31 us (5%)
  starting transfers between devices  19.4 us (3%)
  between operations  14 us (2%)
    dot_general x20, matrix products, apply_form(): return jnp.einsum(form, table, values, precision=lax.Precision.HIGHEST)  200 us
    unnamed x3, waiting for transfers between devices  161 us
    all_gather x1, waiting for transfers between devices, local(): lax.all_gather(gated, 'tp', axis=0, tiled=True)  54.5 us
    all_to_all x1, waiting for transfers between devices, local(): lax.all_to_all(spec_re.astype(jnp.bfloat16), 'ctx', split_axis=1, concat_...  24.1 us
    convert_element_type x4, local copies, waits for them, and re-layouts, local(): spec_re, spec_im = (lax.all_to_all(spec_re.astype(jnp.bfloat16), 'ctx', s...  19.6 us
    all_to_all x1, waiting for transfers between devices, exchange_blocks(): received = lax.all_to_all(jnp.stack(cells), axis, 0, 0)  17.2 us
    unnamed x16, other arithmetic  13.1 us
    convert_element_type x1, local copies, waits for them, and re-layouts, local(): conv = lax.psum_scatter((apply_form('nj,cjm->ncm', row_re, back_re) - app...  13 us
  transfers between devices with their start and end apart: 5, of which 5 were waited for; matrix products, arithmetic and copies ran while one was open for 5% of the time, Pallas kernels for 0%

profile of v1, /device:TPU:1, one launch (start us, length us, event | category | flops | bytes accessed | tf_op | source)
XLA Modules:
  0.0 587.9 jit_solution(5155563742916087325)
XLA Ops:
  6.5 2.0 fusion.52
  8.5 0.7 bitcast_dynamic-update-slice_fusion.14
  9.2 0.7 bitcast_dynamic-update-slice_fusion.13
  9.9 0.7 bitcast_dynamic-update-slice_fusion.12
  10.5 0.7 bitcast_dynamic-update-slice_fusion.11
  11.8 0.7 bitcast_dynamic-update-slice_fusion.9
  12.5 0.7 bitcast_dynamic-update-slice_fusion.8
  13.1 0.7 bitcast_dynamic-update-slice_fusion.7
  14.4 0.7 bitcast_dynamic-update-slice_fusion.5
  15.1 0.7 bitcast_dynamic-update-slice_fusion.4
  15.8 0.7 bitcast_dynamic-update-slice_fusion.3
  16.4 0.7 bitcast_dynamic-update-slice_fusion.2
  17.1 0.7 bitcast_dynamic-update-slice_fusion.1
  17.7 0.7 bitcast_dynamic-update-slice_fusion
  18.4 0.7 fusion.101
  19.1 9.1 %all-to-all-start = ((bf16[16,8,1,4096]{3,1,2,0:T(8,128)(2,1)}), bf16[16,8,1,4096]{3,1,2,0:T(8,128)(2,1)S(1)}, u32[]{:S(2)}, u32[]{:S(2)}) async-start(bf16[16,8,1,4096]{3,1,2,0:T(8,128)(2,1)} %fusion.101), calls=%async_computation | async-start | bytes 2097152 | tf_op jit(solution)/shard_map/all_to_all | solution.py:12
  28.4 17.2 %all-to-all-done = bf16[16,8,1,4096]{3,1,2,0:T(8,128)(2,1)S(1)} async-done(((bf16[16,8,1,4096]{3,1,2,0:T(8,128)(2,1)}), bf16[16,8,1,4096]{3,1,2,0:T(8,128)(2,1)S(1)}, u32[]{:S(2)}, u32[]{:S(2)}) %all-to-all-start) | async-done | bytes 1048608 | tf_op jit(solution)/shard_map/all_to_all | solution.py:12
  45.5 2.0 fusion.1
  47.6 2.5 copy.595
  50.1 4.2 all-to-all-start.1
  54.4 2.0 fusion.2
  56.4 2.5 copy.597
  58.9 24.1 %all-to-all-done.1 = bf16[8,32,4096]{2,0,1:T(8,128)(2,1)S(1)} async-done(((bf16[8,32,4096]{2,0,1:T(8,128)(2,1)}), bf16[8,32,4096]{2,0,1:T(8,128)(2,1)S(1)}, u32[]{:S(2)}, u32[]{:S(2)}) %all-to-all-start.1) | async-done | bytes 2097184 | tf_op jit(solution)/shard_map/all_to_all | solution.py:81
  83.0 5.5 all-to-all-start.2
  89.0 8.9 %fusion.77 = (f32[2,65536]{1,0:T(2,128)S(1)}, f32[2,65536]{1,0:T(2,128)S(1)}) fusion(s32[2]{0:T(128)S(1)} %pad_add_fusion.1), kind=kLoop, calls=%fused_computation.140 | loop fusion | flops 1835008 | bytes 1048584 | tf_op jit(solution)/shard_map/cos | solution.py:19
  97.9 1.0 multiply_cosine_fusion.6
  98.9 0.8 copy.607
  99.7 1.0 multiply_sine_fusion.6
  100.7 0.9 copy.608
  101.6 1.7 multiply_sine_fusion.7
  103.3 2.1 fusion.81
  105.4 4.8 copy.647
  110.2 4.9 reshape.224
  115.1 2.0 all-to-all-done.2
  117.2 4.8 copy.646
  122.0 5.1 reshape.225
  127.1 21.0 %fusion.34 = f32[8,2,128,512]{3,2,1,0:T(8,128)S(1)} fusion(f32[8,2,512,128]{3,2,1,0:T(8,128)} %reshape.225, f32[8,2,512,128]{3,2,1,0:T(8,128)} %reshape.224, f32[2,512,128]{2,1,0:T(8,128)S(1)} %get-tuple-element.8, f32[2,512,128]{2,1,0:T(8,128)S(1)} %get-tuple-element.7), kind=kOutput, calls=%fused_computation.90 | convolution fusion | flops 6449266688 | bytes 13631488 | tf_op jit(solution)/shard_map/cb,...ba->...ca/dot_general | solution.py:23
  148.1 17.5 %fusion.32 = f32[8,2,128,512]{3,2,1,0:T(8,128)S(1)} fusion(f32[8,2,512,128]{3,2,1,0:T(8,128)S(1)} %copy-done.2, f32[8,2,512,128]{3,2,1,0:T(8,128)S(1)} %copy-done.1, f32[2,512,128]{2,1,0:T(8,128)S(1)} %get-tuple-element.8, f32[2,512,128]{2,1,0:T(8,128)S(1)} %get-tuple-element.7), kind=kOutput, calls=%fused_computation.88 | convolution fusion | flops 6449266688 | bytes 13631488 | tf_op jit(solution)/shard_map/cb,...ba->...ca/dot_general | solution.py:23
  165.6 17.5 %convolution_subtract_fusion.2 = f32[8,2,128,512]{3,2,1,0:T(8,128)S(1)} fusion(f32[8,2,128,512]{3,2,1,0:T(8,128)S(1)} %fusion.34, f32[8,2,512,128]{3,2,1,0:T(8,128)S(1)} %copy-done.2, f32[8,2,512,128]{3,2,1,0:T(8,128)S(1)} %copy-done.1, f32[2,512,128]{2,1,0:T(8,128)S(1)} %get-tuple-element.8, f32[2,512,128]{2,1,0:T(8,128)S(1)} %get-tuple-element.7), kind=kOutput, calls=%fused_computation.50 | convolution fusion | flops 6450315264 | bytes 17825792 | tf_op jit(solution)/shard_map/cb,...ba->...ca/dot_general | solution.py:23
  183.1 17.5 %convolution_add_fusion.1 = f32[8,2,128,512]{3,2,1,0:T(8,128)S(1)} fusion(f32[8,2,128,512]{3,2,1,0:T(8,128)S(1)} %fusion.32, f32[8,2,512,128]{3,2,1,0:T(8,128)S(1)} %copy-done.2, f32[8,2,512,128]{3,2,1,0:T(8,128)S(1)} %copy-done.1, f32[2,512,128]{2,1,0:T(8,128)S(1)} %get-tuple-element.8, f32[2,512,128]{2,1,0:T(8,128)S(1)} %get-tuple-element.7), kind=kOutput, calls=%fused_computation.49 | convolution fusion | flops 6450315264 | bytes 17825792 | tf_op jit(solution)/shard_map/cb,...ba->...ca/dot_general | solution.py:23
  200.7 7.4 %fusion.18 = f32[8,2,512,128]{3,2,1,0:T(8,128)S(1)} fusion(f32[8,2,128,512]{3,2,1,0:T(8,128)S(1)} %convolution_add_fusion.1, f32[8,2,128,512]{3,2,1,0:T(8,128)S(1)} %convolution_subtract_fusion.2, f32[512,128]{0,1:T(8,128)S(1)} %get-tuple-element.13, f32[512,128]{0,1:T(8,128)S(1)} %copy-done.7), kind=kOutput, calls=%fused_computation.72 | convolution fusion | flops 1613987840 | bytes 13107200 | tf_op jit(solution)/shard_map/...ca,ad->...cd/dot_general | solution.py:23
  208.1 7.4 %fusion.14 = f32[8,2,512,128]{3,2,1,0:T(8,128)S(1)} fusion(f32[8,2,128,512]{3,2,1,0:T(8,128)S(1)} %convolution_add_fusion.1, f32[8,2,128,512]{3,2,1,0:T(8,128)S(1)} %convolution_subtract_fusion.2, f32[512,128]{0,1:T(8,128)S(1)} %get-tuple-element.13, f32[512,128]{0,1:T(8,128)S(1)} %copy-done.7), kind=kOutput, calls=%fused_computation.71 | convolution fusion | flops 1613987840 | bytes 13107200 | tf_op jit(solution)/shard_map/...ca,ad->...cd/dot_general | solution.py:23
  215.5 7.2 %convolution_subtract_fusion.1 = f32[8,2,512,128]{3,2,1,0:T(8,128)S(1)} fusion(f32[8,2,512,128]{3,2,1,0:T(8,128)S(1)} %fusion.18, f32[8,2,128,512]{3,2,1,0:T(8,128)S(1)} %convolution_add_fusion.1, f32[8,2,128,512]{3,2,1,0:T(8,128)S(1)} %convolution_subtract_fusion.2, f32[512,128]{0,1:T(8,128)S(1)} %get-tuple-element.13, f32[512,128]{0,1:T(8,128)S(1)} %copy-done.7), kind=kOutput, calls=%fused_computation.48 | convolution fusion | flops 1615036416 | bytes 17301504 | tf_op jit(solution)/shard_map/...ca,ad->...cd/dot_general | solution.py:23
  222.7 7.6 %convolution_add_fusion = f32[8,2,512,128]{3,2,1,0:T(8,128)S(1)} fusion(f32[8,2,512,128]{3,2,1,0:T(8,128)S(1)} %fusion.14, f32[8,2,128,512]{3,2,1,0:T(8,128)S(1)} %convolution_add_fusion.1, f32[8,2,128,512]{3,2,1,0:T(8,128)S(1)} %convolution_subtract_fusion.2, f32[512,128]{0,1:T(8,128)S(1)} %get-tuple-element.13, f32[512,128]{0,1:T(8,128)S(1)} %copy-done.7), kind=kOutput, calls=%fused_computation.47 | convolution fusion | flops 1615036416 | bytes 17301504 | tf_op jit(solution)/shard_map/...ca,ad->...cd/dot_general | solution.py:23
  230.8 2.1 fusion.106
  233.0 2.1 fusion.104
  235.1 2.1 convolution_subtract_fusion.3
  237.3 2.3 convolution_add_fusion.2
  239.6 10.6 %fusion.28 = f32[4,2,128,512]{3,2,1,0:T(8,128)S(1)} fusion(f32[4,2,512,128]{3,2,1,0:T(8,128)S(1)} %convolution_add_fusion.2, f32[4,2,512,128]{3,2,1,0:T(8,128)S(1)} %convolution_subtract_fusion.3, f32[512,128]{1,0:T(8,128)S(1)} %copy-done.9, f32[512,128]{1,0:T(8,128)S(1)} %copy-done.8), kind=kOutput, calls=%fused_computation.84 | convolution fusion | flops 3226468352 | bytes 6815744 | tf_op jit(solution)/shard_map/bc,...ca->...ba/dot_general | solution.py:23
  250.2 11.8 %fusion.26 = f32[4,2,128,512]{3,2,1,0:T(8,128)} fusion(f32[4,2,512,128]{3,2,1,0:T(8,128)S(1)} %convolution_add_fusion.2, f32[4,2,512,128]{3,2,1,0:T(8,128)S(1)} %convolution_subtract_fusion.3, f32[512,128]{1,0:T(8,128)S(1)} %copy-done.9, f32[512,128]{1,0:T(8,128)S(1)} %copy-done.8), kind=kOutput, calls=%fused_computation.82 | convolution fusion | flops 3226468352 | bytes 6815744 | tf_op jit(solution)/shard_map/bc,...ca->...ba/dot_general | solution.py:23
  262.0 12.2 %subtract_bitcast_fusion = f32[4,2,512,128]{2,3,1,0:T(8,128)} fusion(f32[4,2,128,512]{3,2,1,0:T(8,128)S(1)} %fusion.28, f32[4,2,512,128]{3,2,1,0:T(8,128)S(1)} %convolution_add_fusion.2, f32[4,2,512,128]{3,2,1,0:T(8,128)S(1)} %convolution_subtract_fusion.3, f32[512,128]{1,0:T(8,128)S(1)} %copy-done.9, f32[512,128]{1,0:T(8,128)S(1)} %copy-done.8), kind=kOutput, calls=%fused_computation.61 | convolution fusion | flops 3226992640 | bytes 8912896 | tf_op jit(solution)/shard_map/bc,...ca->...ba/dot_general | solution.py:23
  274.2 3.0 copy.611
  277.2 4.4 reshape.222
  281.5 14.2 %add_bitcast_fusion = f32[4,2,512,128]{2,3,1,0:T(8,128)} fusion(f32[4,2,128,512]{3,2,1,0:T(8,128)} %fusion.26, f32[4,2,512,128]{3,2,1,0:T(8,128)} %copy-done.3, f32[4,2,512,128]{3,2,1,0:T(8,128)S(1)} %convolution_subtract_fusion.3, f32[512,128]{1,0:T(8,128)} %copy.608, f32[512,128]{1,0:T(8,128)S(1)} %copy-done.8), kind=kOutput, calls=%fused_computation.59 | convolution fusion | flops 3226992640 | bytes 8912896 | tf_op jit(solution)/shard_map/bc,...ca->...ba/dot_general | solution.py:23
  295.7 3.0 copy.614
  298.7 4.4 reshape.223
  303.1 17.6 %fusion.9 = f32[16,4,65536]{2,0,1:T(8,128)S(1)} fusion(f32[4,2,65536]{2,1,0:T(2,128)} %reshape.223, f32[4,2,65536]{2,1,0:T(2,128)S(1)} %copy-done.4, f32[2,65536]{1,0:T(2,128)S(1)} %get-tuple-element.10, f32[2,65536]{1,0:T(2,128)S(1)} %get-tuple-element.9, s32[2]{0:T(128)S(1)} %pad_add_fusion.1), kind=kOutput, calls=%fused_computation.55 | convolution fusion | flops 102760896 | bytes 22020104 | tf_op jit(solution)/shard_map/nj,cjm->ncm/dot_general | solution.py:23
  320.7 18.1 %fusion = bf16[16,4,65536]{2,0,1:T(8,128)(2,1)S(1)} fusion(f32[16,4,65536]{2,0,1:T(8,128)S(1)} %fusion.9, f32[4,2,65536]{2,1,0:T(2,128)S(1)} %copy-done.5, f32[4,2,65536]{2,1,0:T(2,128)S(1)} %copy-done.4, f32[2,65536]{1,0:T(2,128)S(1)} %get-tuple-element.10, f32[2,65536]{1,0:T(2,128)S(1)} %get-tuple-element.9, s32[2]{0:T(128)S(1)} %pad_add_fusion.1), kind=kOutput, calls=%fused_computation.1 | convolution fusion | flops 111149504 | bytes 30408712 | tf_op jit(solution)/shard_map/nj,cjm->ncm/dot_general | solution.py:23
  338.8 13.0 %copy.615 = bf16[16,4,65536]{2,1,0:T(4,128)(2,1)} copy(bf16[16,4,65536]{2,0,1:T(8,128)(2,1)S(1)} %fusion) | data formatting | bytes 16777216 | tf_op jit(solution)/shard_map/convert_element_type | solution.py:111
  353.1 160.9 %all-reduce.3.cloned.1.call-done = bf16[16,4,65536]{2,1,0:T(4,128)(2,1)} async-done(((bf16[16,4,65536]{2,1,0:T(4,128)(2,1)}), bf16[16,4,65536]{2,1,0:T(4,128)(2,1)}) %all-reduce.3.cloned.1.call-update) | async-done | bytes 8388624
  514.0 3.3 fusion.56
  517.3 54.5 %all-gather.3.cloned.1.call-done = bf16[8,4,65536]{2,1,0:T(4,128)(2,1)} async-done(((bf16[1,4,65536]{2,1,0:T(4,128)(2,1)}), bf16[8,4,65536]{2,1,0:T(4,128)(2,1)}) %all-gather.3.cloned.1.call-update) | async-done | bytes 4194320 | tf_op jit(solution)/shard_map/all_gather | solution.py:124
  571.8 5.2 reshape.230
  577.0 3.8 convolution_convert_fusion
  (45 shorter events, 3.9 us)
Async XLA Ops:
  6.5 570.5 %copy-start = (bf16[32,32]{1,0:T(8,128)(2,1)S(1)}, bf16[32,32]{1,0:T(8,128)(2,1)}, u32[]{:S(2)}) copy-start(bf16[32,32]{1,0:T(8,128)(2,1)} %param.11) | copy-start | bytes 6148
  19.1 26.5 %all-to-all-start = ((bf16[16,8,1,4096]{3,1,2,0:T(8,128)(2,1)}), bf16[16,8,1,4096]{3,1,2,0:T(8,128)(2,1)S(1)}, u32[]{:S(2)}, u32[]{:S(2)}) async-start(bf16[16,8,1,4096]{3,1,2,0:T(8,128)(2,1)} %fusion.101), calls=%async_computation | async-start | bytes 2097152 | tf_op jit(solution)/shard_map/all_to_all | solution.py:12
  50.1 32.9 %all-to-all-start.1 = ((bf16[8,32,4096]{2,0,1:T(8,128)(2,1)}), bf16[8,32,4096]{2,0,1:T(8,128)(2,1)S(1)}, u32[]{:S(2)}, u32[]{:S(2)}) async-start(bf16[8,32,4096]{2,0,1:T(8,128)(2,1)} %copy.595), calls=%async_computation.1 | async-start | bytes 4194304 | tf_op jit(solution)/shard_map/all_to_all | solution.py:81
  83.0 18.6 %copy-start.6 = (bf16[8,32,4096]{2,0,1:T(8,128)(2,1)}, bf16[8,32,4096]{2,0,1:T(8,128)(2,1)S(1)}, u32[]{:S(2)}) copy-start(bf16[8,32,4096]{2,0,1:T(8,128)(2,1)S(1)} %all-to-all-done.1) | copy-start | bytes 6291460
  83.0 34.2 %all-to-all-start.2 = ((bf16[8,32,4096]{2,0,1:T(8,128)(2,1)}), bf16[8,32,4096]{2,0,1:T(8,128)(2,1)}, u32[]{:S(2)}, u32[]{:S(2)}) async-start(bf16[8,32,4096]{2,0,1:T(8,128)(2,1)} %copy.597), calls=%async_computation.2 | async-start | bytes 4194304 | tf_op jit(solution)/shard_map/all_to_all | solution.py:84
  88.5 425.6 %all-reduce.3.cloned.1.call-start = ((), (), s32[]{:S(2)}) async-start(), calls=%async_computation.4 | async-start | bytes 16777216
  127.1 21.1 %copy-start.1 = (f32[8,2,512,128]{3,2,1,0:T(8,128)S(1)}, f32[8,2,512,128]{3,2,1,0:T(8,128)}, u32[]{:S(2)}) copy-start(f32[8,2,512,128]{3,2,1,0:T(8,128)} %reshape.224) | copy-start | bytes 12582916
  127.1 21.1 %copy-start.2 = (f32[8,2,512,128]{3,2,1,0:T(8,128)S(1)}, f32[8,2,512,128]{3,2,1,0:T(8,128)}, u32[]{:S(2)}) copy-start(f32[8,2,512,128]{3,2,1,0:T(8,128)} %reshape.225) | copy-start | bytes 12582916
  183.1 17.6 %copy-start.7 = (f32[512,128]{0,1:T(8,128)S(1)}, f32[512,128]{0,1:T(8,128)}, u32[]{:S(2)}) copy-start(f32[512,128]{0,1:T(8,128)} %get-tuple-element.14) | copy-start | bytes 786436
  237.3 2.3 copy-start.8
  237.3 2.3 copy-start.9
  239.6 22.4 %copy-start.3 = (f32[4,2,512,128]{3,2,1,0:T(8,128)}, f32[4,2,512,128]{3,2,1,0:T(8,128)S(1)}, u32[]{:S(2)}) copy-start(f32[4,2,512,128]{3,2,1,0:T(8,128)S(1)} %convolution_add_fusion.2) | copy-start | bytes 6291460
  295.7 7.5 %copy-start.4 = (f32[4,2,65536]{2,1,0:T(2,128)S(1)}, f32[4,2,65536]{2,1,0:T(2,128)}, u32[]{:S(2)}) copy-start(f32[4,2,65536]{2,1,0:T(2,128)} %reshape.222) | copy-start | bytes 6291460
  303.1 17.6 %copy-start.5 = (f32[4,2,65536]{2,1,0:T(2,128)S(1)}, f32[4,2,65536]{2,1,0:T(2,128)}, u32[]{:S(2)}) copy-start(f32[4,2,65536]{2,1,0:T(2,128)} %reshape.223) | copy-start | bytes 6291460
  351.8 0.7 copy-start.14
  351.9 162.2 %copy-start.10 = (bf16[4,65536]{1,0:T(4,128)(2,1)S(1)}, bf16[4,65536]{1,0:T(4,128)(2,1)}, u32[]{:S(2)}) copy-start(bf16[4,65536]{1,0:T(4,128)(2,1)} %param.8) | copy-start | bytes 1572868
  351.9 162.2 %copy-start.11 = (bf16[4,65536]{1,0:T(4,128)(2,1)S(1)}, bf16[4,65536]{1,0:T(4,128)(2,1)}, u32[]{:S(2)}) copy-start(bf16[4,65536]{1,0:T(4,128)(2,1)} %param.7) | copy-start | bytes 1572868
  351.9 162.2 %copy-start.12 = (bf16[4,65536]{1,0:T(4,128)(2,1)S(1)}, bf16[4,65536]{1,0:T(4,128)(2,1)}, u32[]{:S(2)}) copy-start(bf16[4,65536]{1,0:T(4,128)(2,1)} %param.6) | copy-start | bytes 1572868
  351.9 162.2 %copy-start.13 = (f32[4]{0:T(128)S(1)}, f32[4]{0:T(128)}, u32[]{:S(2)}) copy-start(f32[4]{0:T(128)} %param.10) | copy-start | bytes 52
  351.9 219.9 %all-gather.3.cloned.1.call-start = ((), (), s32[]{:S(2)}) async-start(), calls=%async_computation.3 | async-start | bytes 4718592 | tf_op jit(solution)/shard_map/all_gather | solution.py:124
Sparse Core Ops, SparseCore 0:
  352.0 161.9 all-reduce.2
  517.4 54.2 all-gather.2
